TPU v7x, 512 devices: a whole 4x8x8 slice. The times are simulated.
512 devices in a mesh: leaf: 32 (over y, x), col: 16 (over z, core).
Axes of the slice: x: 4, y: 8, z: 8, core: 2. Of those that a mesh axis runs over, the one named last changes fastest.
Arguments:
- points: float32 [3, 262144], P(None, ('leaf', 'col'))
- point_ids: int32 [262144], P(('leaf', 'col')), may hold values from 0 to 1048575, as said below
- signs: int32 [262144], P(('leaf', 'col')), may hold values from 0 to 1
- hadamard_sample_rows: int32 [512], replicated, may hold values from 0 to 1048575, as said below
- samples: bfloat16 [262144, 512], P(('leaf', 'col')), may hold values from -6 to 6
- skeleton: int32 [60, 128], replicated, may hold values from 0 to 8191, as said below
- ranks: int32 [60], replicated, may hold values from 64 to 128, as said below
Outputs:
- leaf_basis: bfloat16 [262144, 128], P(('leaf', 'col'))
- top_sample: float32 [512, 512], P('leaf', 'col')
- top_omega: float32 [512, 512], P('leaf', 'col')
Inputs may be any that keep to these rules, and one draw needn't show every extreme that they name: `point_ids`: increasing and distinct; the first is 0 and the last 1048575. `hadamard_sample_rows`: increasing and distinct; the first is 0 and the last 1048575. `skeleton`: each row holds distinct indices; in the first 32 rows (leaves) they are below 8192, in the others below 256; entry i of a leaf row lies in [i * 64, (i + 1) * 64). `ranks`: some node has rank 128 and some other node rank 128 / 2.
All inputs are finite; a program needn't handle non-finite values.
Results may differ from a plain program's by a relative error of at most 0.0018.
Values sent between devices are 32-bit elements; how exact they have to be, the bound alone decides.
A program may use at most 64 MiB of HBM per device.

v0:
```python
import jax
import jax.numpy as jnp
from jax import lax
from jax.sharding import PartitionSpec as P

NTOTAL = 1048576
KERNEL_SCALE = 1.0
OMEGA_UNIT = 0.0625
RIDGE = 0.25
HIGH = lax.Precision.HIGHEST


def swapped(value, axis, bit):
    mask = 2**bit
    pairs = [(source, source ^ mask) for source in range(lax.axis_size(axis))]
    return lax.ppermute(value, axis, pairs)


def omega_rows(tags, hadamard_sample_rows, bit_count):
    powers = jnp.array([1 << shift for shift in range(bit_count)], dtype=jnp.int32)
    row_bits = (tags[0][:, None] // powers[None, :] % 2).astype(jnp.float32)
    col_bits = (hadamard_sample_rows[None, :] // powers[:, None] % 2).astype(jnp.float32)
    counted = jnp.dot(row_bits, col_bits, precision=HIGH)
    parity = counted - 2.0 * jnp.floor(0.5 * counted)
    flips = (2 * tags[1] - 1).astype(jnp.float32)
    return (1.0 - 2.0 * parity) * flips[:, None] * OMEGA_UNIT


def kernel_tile(left, right):
    squared_distance = jnp.zeros((left.shape[1], right.shape[1]), jnp.float32)
    for axis_k in range(3):
        offset = left[axis_k][:, None] - right[axis_k][None, :]
        squared_distance = squared_distance + offset * offset
    return jnp.exp(-KERNEL_SCALE * squared_distance)


def ridge_fit(picked, gram, rank):
    shift = RIDGE * jnp.trace(gram) / rank.astype(jnp.float32) + 1e-06
    ident = jnp.eye(gram.shape[0], dtype=jnp.float32)
    factor = jnp.linalg.cholesky(gram + shift * ident)
    return jax.scipy.linalg.cho_solve((factor, True), picked)


def local(points, point_ids, signs, hadamard_sample_rows, samples, skeleton, ranks):
    leaf_count = lax.axis_size("leaf")
    col_count = lax.axis_size("col")
    leaf_pos = lax.axis_index("leaf")
    col_pos = lax.axis_index("col")
    rows = points.shape[1]
    width = samples.shape[1]
    rank_limit = skeleton.shape[1]
    bit_count = NTOTAL.bit_length() - 1
    tags = jnp.stack([point_ids, signs])
    own_omega = omega_rows(tags, hadamard_sample_rows, bit_count)
    distant_points = lax.all_gather(points, "col", axis=1, tiled=True)
    far_tags = lax.all_gather(tags, "col", axis=1, tiled=True)
    block_omega = omega_rows(far_tags, hadamard_sample_rows, bit_count).astype(jnp.bfloat16)
    tile = kernel_tile(points, distant_points).astype(jnp.bfloat16)
    near = jnp.dot(tile, block_omega, preferred_element_type=jnp.float32)
    residue = samples.astype(jnp.float32) - near
    positions = jnp.arange(rank_limit, dtype=jnp.int32)
    leaf_skel = skeleton[leaf_pos] - col_pos * rows
    leaf_rank = ranks[leaf_pos]
    keep = (positions < leaf_rank).astype(jnp.float32)
    chooser = (leaf_skel[:, None] == jnp.arange(rows, dtype=jnp.int32)[None, :]).astype(jnp.float32)
    part_picked = jnp.dot(chooser, residue, precision=HIGH) * keep[:, None]
    part_spots = jnp.dot(points, chooser.T, precision=HIGH)
    picked, spots = lax.psum((part_picked, part_spots), "col")
    gram = jnp.dot(picked, picked.T, precision=HIGH)
    fitted = ridge_fit(picked, gram, leaf_rank)
    basis = jnp.dot(residue, fitted.T, precision=HIGH)
    projected = lax.psum(jnp.dot(basis.T, own_omega, precision=HIGH), "col")
    leaf_basis = basis.astype(jnp.bfloat16)
    span = width // col_count
    base = 0
    for level in range(1, 4):
        child_base = base
        base = base + (leaf_count >> level - 1)
        sibling_selected, other_proj, other_spots = swapped(
            (picked, projected, spots), "leaf", level - 1
        )
        is_left = leaf_pos // (1 << level - 1) % 2 == 0
        left_picked = jnp.where(is_left, picked, sibling_selected)
        right_picked = jnp.where(is_left, sibling_selected, picked)
        left_proj = jnp.where(is_left, projected, other_proj)
        right_proj = jnp.where(is_left, other_proj, projected)
        left_positions = jnp.where(is_left, spots, other_spots)
        right_spots = jnp.where(is_left, other_spots, spots)
        pair_index = leaf_pos // (1 << level)
        left_keep = (positions < ranks[child_base + 2 * pair_index]).astype(jnp.float32)
        right_keep = (positions < ranks[child_base + 2 * pair_index + 1]).astype(jnp.float32)
        cross = kernel_tile(left_positions, right_spots)
        upper = (left_picked - jnp.dot(cross, right_proj, precision=HIGH)) * left_keep[:, None]
        lower = (right_picked - jnp.dot(cross.T, left_proj, precision=HIGH)) * right_keep[:, None]
        candidates = jnp.concatenate([upper, lower], 0)
        stacked = jnp.concatenate([left_proj, right_proj], 0)
        cand_spots = jnp.concatenate([left_positions, right_spots], 1)
        node_skel = skeleton[base + pair_index]
        node_rank = ranks[base + pair_index]
        node_keep = (positions < node_rank).astype(jnp.float32)
        selector = (
            node_skel[:, None] == jnp.arange(2 * rank_limit, dtype=jnp.int32)[None, :]
        ).astype(jnp.float32)
        new_picked = jnp.dot(selector, candidates, precision=HIGH) * node_keep[:, None]
        new_spots = jnp.dot(cand_spots, selector.T, precision=HIGH)
        gram = jnp.dot(new_picked, new_picked.T, precision=HIGH)
        fitted = ridge_fit(new_picked, gram, node_rank)
        parent_basis = jnp.dot(candidates, fitted.T, precision=HIGH)
        projected = jnp.dot(parent_basis.T, stacked, precision=HIGH)
        picked = new_picked
        spots = new_spots
    picked = lax.dynamic_slice_in_dim(picked, col_pos * span, span, 1)
    projected = lax.dynamic_slice_in_dim(projected, col_pos * span, span, 1)
    share = rank_limit // 8
    top_sample = lax.dynamic_slice_in_dim(picked, leaf_pos % 8 * share, share, 0)
    top_omega = lax.dynamic_slice_in_dim(projected, leaf_pos % 8 * share, share, 0)
    return (leaf_basis, top_sample, top_omega)


def solution(mesh):
    placed = (
        P(None, ("leaf", "col")),
        P(("leaf", "col")),
        P(("leaf", "col")),
        P(),
        P(("leaf", "col"), None),
        P(),
        P(),
    )
    return jax.shard_map(
        local,
        mesh=mesh,
        in_specs=placed,
        out_specs=(P(("leaf", "col"), None), P("leaf", "col"), P("leaf", "col")),
        check_vma=False,
    )
```

profile of v0, /device:TPU:2, one launch (start us, length us, event | category | flops | bytes accessed | tf_op | source)
XLA Modules:
  0.0 488.6 jit_solution(7445075124836231805)
XLA Ops:
  7.2 23.8 %all_gather.6 = f32[3,8192]{1,0:T(4,128)S(1)} all-gather(f32[3,512]{1,0:T(4,128)} %param.14), channel_id=1, replica_groups=mesh['leaf'=32,'col'=16] {'col'}, dimensions={1}, use_global_device_ids=true | all-gather | bytes 104448 | tf_op jit(solution)/shard_map/all_gather | solution.py:55
  31.0 0.8 fusion.198
  31.8 0.7 pad_add_fusion
  32.5 14.6 %all_gather.7 = s32[2,8192]{1,0:T(2,128)S(1)} all-gather(s32[2,512]{1,0:T(2,128)S(1)} %pad_add_fusion), channel_id=1, replica_groups=mesh['leaf'=32,'col'=16] {'col'}, dimensions={1}, use_global_device_ids=true | all-gather | bytes 69632 | tf_op jit(solution)/shard_map/all_gather | solution.py:56
  47.2 0.7 compare_reduce_fusion
  48.0 1.7 fusion.199
  49.8 0.7 compare_convert_fusion.9
  50.4 0.8 fusion.165
  51.2 29.2 %multiply_convert_fusion = bf16[8192,512]{1,0:T(8,128)(2,1)S(1)} fusion(f32[8192]{0:T(1024)S(1)} %bitcast.150, s32[20]{0:T(128)} %constant.260.clone, s32[8192]{0:T(1024)S(1)} %bitcast.146, pred[8192]{0:T(1024)(128)(4,1)S(1)} %sign_compare_fusion, s32[512]{0:T(512)} %param.17, pred[512]{0:T(512)(128)(4,1)S(1)} %compare_reduce_fusion), kind=kOutput, calls=%fused_computation | convolution fusion | flops 1047515136 | bytes 8464976 | tf_op jit(solution)/shard_map/dot_general | solution.py:23
  80.5 6.7 %fusion.8 = f32[512,512]{1,0:T(8,128)S(1)} fusion(bf16[8192,512]{1,0:T(8,128)(2,1)S(1)} %multiply_convert_fusion, f32[8192]{0:T(1024)S(1)} %bitcast.148, f32[512]{0:T(512)S(1)} %bitcast.156, f32[8192]{0:T(1024)S(1)} %bitcast.149, f32[512]{0:T(512)S(1)} %bitcast.155, f32[8192]{0:T(1024)S(1)} %bitcast.147, f32[512]{0:T(512)S(1)} %bitcast.154, ...), kind=kOutput, calls=%fused_computation.10 | convolution fusion | flops 4337434624 | bytes 10065920 | tf_op jit(solution)/shard_map/dot_general | solution.py:59
  87.2 1.2 convolution_multiply_fusion.3
  88.8 25.2 %psum.22 = f32[3,128]{1,0:T(4,128)S(1)} all-reduce(f32[3,128]{1,0:T(4,128)S(1)} %convolution_bitcast_fusion), channel_id=1, replica_groups=mesh['leaf'=32,'col'=16] {'col'}, use_global_device_ids=true, to_apply=%region_4.8 | all-reduce | flops 384 | bytes 3072 | tf_op jit(solution)/shard_map/psum | solution.py:68
  114.0 2.8 collective-permute-start.1
  117.5 0.6 compare_convert_fusion.6
  118.8 0.6 compare_convert_fusion.7
  119.5 4.1 fusion.54
  124.1 0.7 compare_convert_fusion.4
  125.4 0.7 compare_convert_fusion.3
  126.1 0.7 compare_convert_fusion.1
  126.8 0.7 compare_convert_fusion.2
  127.4 0.7 compare_convert_fusion
  129.5 72.7 %all-reduce.3.cloned.1.call-done = f32[128,512]{1,0:T(8,128)} async-done(((f32[128,512]{1,0:T(8,128)}), f32[128,512]{1,0:T(8,128)}) %all-reduce.3.cloned.1.call-update) | async-done | bytes 262160 | tf_op jit(solution)/shard_map/psum | solution.py:68
  202.1 2.1 select_reduce_fusion.7
  205.0 11.7 %cholesky.74 = f32[128,128]{1,0:T(8,128)S(1)} custom-call(f32[128,128]{1,0:T(8,128)S(1)} %fusion.94), custom_call_target="Cholesky" | custom-call | tf_op jit(solution)/shard_map/jit(cholesky)/cholesky | solution.py:40
  216.8 0.6 compare_reduce_fusion.4
  217.4 0.7 fusion.71
  218.1 9.8 %custom-call.10 = f32[1,128,128]{1,2,0:T(8,128)S(1)} custom-call(f32[1,128,128]{2,1,0:T(8,128)S(1)} %fusion.71), custom_call_target="InvertDiagBlocksLowerTriangular" | custom-call | tf_op jit(solution)/shard_map/jit(_cho_solve)/triangular_solve | solution.py:41
  227.9 1.4 fusion.92
  229.7 1.8 fusion.200
  231.5 1.8 fusion.9
  233.5 4.0 collective-permute-start.4
  237.5 111.8 %all-reduce.5.cloned.1.call-done = f32[128,512]{1,0:T(8,128)} async-done(((f32[128,512]{1,0:T(8,128)}), f32[128,512]{1,0:T(8,128)}) %all-reduce.5.cloned.1.call-update) | async-done | bytes 262160 | tf_op jit(solution)/shard_map/psum | solution.py:72
  349.3 2.5 collective-permute-start.2
  351.8 3.4 collective-permute-start
  355.2 5.4 %collective-permute-done.2 = f32[128,512]{1,0:T(8,128)S(1)} collective-permute-done((f32[128,512]{1,0:T(8,128)}, f32[128,512]{1,0:T(8,128)S(1)}, u32[]{:S(2)}, u32[]{:S(2)}) %collective-permute-start.2) | collective-permute-done | bytes 262176 | tf_op jit(solution)/shard_map/ppermute | solution.py:16
  360.6 1.0 broadcast_select_fusion.1
  361.6 3.5 collective-permute-done
  365.2 1.5 subtract_multiply_fusion.4
  367.5 1.0 select_reduce_fusion.6
  369.3 11.7 %cholesky.85 = f32[128,128]{1,0:T(8,128)S(1)} custom-call(f32[128,128]{1,0:T(8,128)S(1)} %fusion.89), custom_call_target="Cholesky" | custom-call | tf_op jit(solution)/shard_map/jit(cholesky)/cholesky | solution.py:40
  381.0 0.6 compare_reduce_fusion.3
  381.7 0.7 fusion.72
  382.3 9.8 %custom-call.11 = f32[1,128,128]{1,2,0:T(8,128)S(1)} custom-call(f32[1,128,128]{2,1,0:T(8,128)S(1)} %fusion.72), custom_call_target="InvertDiagBlocksLowerTriangular" | custom-call | tf_op jit(solution)/shard_map/jit(_cho_solve)/triangular_solve | solution.py:41
  394.0 4.0 collective-permute-start.5
  398.0 3.4 collective-permute-start.3
  401.6 3.7 collective-permute-start.7
  405.2 1.3 collective-permute-done.5
  406.6 3.7 collective-permute-done.3
  411.6 1.0 select_reduce_fusion.5
  413.4 11.7 %cholesky.96 = f32[128,128]{1,0:T(8,128)S(1)} custom-call(f32[128,128]{1,0:T(8,128)S(1)} %fusion.84), custom_call_target="Cholesky" | custom-call | tf_op jit(solution)/shard_map/jit(cholesky)/cholesky | solution.py:40
  425.2 0.6 compare_reduce_fusion.2
  425.8 0.7 fusion.73
  426.5 9.8 %custom-call.12 = f32[1,128,128]{1,2,0:T(8,128)S(1)} custom-call(f32[1,128,128]{2,1,0:T(8,128)S(1)} %fusion.73), custom_call_target="InvertDiagBlocksLowerTriangular" | custom-call | tf_op jit(solution)/shard_map/jit(_cho_solve)/triangular_solve | solution.py:41
  438.2 3.4 collective-permute-start.8
  441.6 2.7 collective-permute-start.6
  444.3 4.7 collective-permute-done.8
  449.0 3.1 collective-permute-done.6
  453.4 1.0 select_reduce_fusion.4
  455.3 11.7 %cholesky.107 = f32[128,128]{1,0:T(8,128)S(1)} custom-call(f32[128,128]{1,0:T(8,128)S(1)} %fusion.79), custom_call_target="Cholesky" | custom-call | tf_op jit(solution)/shard_map/jit(cholesky)/cholesky | solution.py:40
  467.0 0.6 compare_reduce_fusion.1
  467.6 0.7 fusion.74
  468.3 9.8 %custom-call.13 = f32[1,128,128]{1,2,0:T(8,128)S(1)} custom-call(f32[1,128,128]{2,1,0:T(8,128)S(1)} %fusion.74), custom_call_target="InvertDiagBlocksLowerTriangular" | custom-call | tf_op jit(solution)/shard_map/jit(_cho_solve)/triangular_solve | solution.py:41
  480.0 0.7 dynamic_slice.64
  480.7 0.7 dynamic_slice.65
  (76 shorter events, 12.0 us)
Async XLA Ops:
  7.2 194.9 %all-reduce.3.cloned.1.call-start = ((), (), s32[]{:S(2)}) async-start(), calls=%async_computation | async-start | bytes 524288 | tf_op jit(solution)/shard_map/psum | solution.py:68
  51.2 29.2 %copy-start.5 = (bf16[512,512]{1,0:T(8,128)(2,1)S(1)}, bf16[512,512]{1,0:T(8,128)(2,1)}, u32[]{:S(2)}) copy-start(bf16[512,512]{1,0:T(8,128)(2,1)} %param.18) | copy-start | bytes 1572868
  80.4 8.1 %copy-start.1 = (f32[3,512]{1,0:T(4,128)S(1)}, f32[3,512]{1,0:T(4,128)}, u32[]{:S(2)}) copy-start(f32[3,512]{1,0:T(4,128)} %param.14) | copy-start | bytes 18436
  80.4 37.1 %copy-start.2 = (s32[512]{0:T(512)S(1)}, s32[512]{0:T(512)}, u32[]{:S(2)}) copy-start(s32[512]{0:T(512)} %param.15) | copy-start | bytes 6148
  80.4 37.1 %copy-start.3 = (s32[512]{0:T(512)S(1)}, s32[512]{0:T(512)}, u32[]{:S(2)}) copy-start(s32[512]{0:T(512)} %param.16) | copy-start | bytes 6148
  80.5 39.0 %copy-start.4 = (s32[512]{0:T(512)S(1)}, s32[512]{0:T(512)}, u32[]{:S(2)}) copy-start(s32[512]{0:T(512)} %param.17) | copy-start | bytes 6148
  80.5 39.0 %copy-start.6 = (s32[20]{0:T(128)S(1)}, s32[20]{0:T(128)}, u32[]{:S(2)}) copy-start(s32[20]{0:T(128)} %constant.260.clone) | copy-start | bytes 244
  88.5 260.9 %all-reduce.5.cloned.1.call-start = ((), (), s32[]{:S(2)}) async-start(), calls=%async_computation.1 | async-start | bytes 524288 | tf_op jit(solution)/shard_map/psum | solution.py:72
  114.0 15.5 %collective-permute-start.1 = (f32[3,128]{1,0:T(4,128)S(1)}, f32[3,128]{1,0:T(4,128)S(1)}, u32[]{:S(2)}, u32[]{:S(2)}) collective-permute-start(f32[3,128]{1,0:T(4,128)S(1)} %psum.22), channel_id=1, source_target_pairs={{0,16},{16,0},{32,48},{48,32},{64,80},{80,64},{96,112},{112,96},{1... | collective-permute-start | bytes 4616 | tf_op jit(solution)/shard_map/ppermute | solution.py:16
  202.1 164.5 %copy-start = (f32[128,512]{1,0:T(8,128)S(1)}, f32[128,512]{1,0:T(8,128)}, u32[]{:S(2)}) copy-start(f32[128,512]{1,0:T(8,128)} %all-reduce.3.cloned.1.call-done) | copy-start | bytes 786436
  233.5 121.7 %collective-permute-start.4 = (f32[3,128]{1,0:T(4,128)S(1)}, f32[3,128]{1,0:T(4,128)S(1)}, u32[]{:S(2)}, u32[]{:S(2)}) collective-permute-start(f32[3,128]{1,0:T(4,128)S(1)} %fusion.66), channel_id=1, source_target_pairs={{0,32},{16,48},{32,0},{48,16},{64,96},{80,112},{96,64},{112,80},{1... | collective-permute-start | bytes 4616 | tf_op jit(solution)/shard_map/ppermute | solution.py:16
  349.3 11.3 %collective-permute-start.2 = (f32[128,512]{1,0:T(8,128)}, f32[128,512]{1,0:T(8,128)S(1)}, u32[]{:S(2)}, u32[]{:S(2)}) collective-permute-start(f32[128,512]{1,0:T(8,128)} %all-reduce.5.cloned.1.call-done), channel_id=1, source_target_pairs={{0,16},{16,0},{32,48},{48,32},{64,80},{80,64},{96,112},{112,96},{1... | collective-permute-start | bytes 786440 | tf_op jit(solution)/shard_map/ppermute | solution.py:16
  351.8 13.3 %collective-permute-start = (f32[128,512]{1,0:T(8,128)}, f32[128,512]{1,0:T(8,128)S(1)}, u32[]{:S(2)}, u32[]{:S(2)}) collective-permute-start(f32[128,512]{1,0:T(8,128)} %all-reduce.3.cloned.1.call-done), channel_id=1, source_target_pairs={{0,16},{16,0},{32,48},{48,32},{64,80},{80,64},{96,112},{112,96},{1... | collective-permute-start | bytes 786440 | tf_op jit(solution)/shard_map/ppermute | solution.py:16
  394.0 12.5 %collective-permute-start.5 = (f32[128,512]{1,0:T(8,128)S(1)}, f32[128,512]{1,0:T(8,128)S(1)}, u32[]{:S(2)}, u32[]{:S(2)}) collective-permute-start(f32[128,512]{1,0:T(8,128)S(1)} %fusion.25), channel_id=1, source_target_pairs={{0,32},{16,48},{32,0},{48,16},{64,96},{80,112},{96,64},{112,80},{1... | collective-permute-start | bytes 786440 | tf_op jit(solution)/shard_map/ppermute | solution.py:16
  398.0 12.3 %collective-permute-start.3 = (f32[128,512]{1,0:T(8,128)S(1)}, f32[128,512]{1,0:T(8,128)S(1)}, u32[]{:S(2)}, u32[]{:S(2)}) collective-permute-start(f32[128,512]{1,0:T(8,128)S(1)} %convolution_multiply_fusion.2), channel_id=1, source_target_pairs={{0,32},{16,48},{32,0},{48,16},{64,96},{80,112},{96,64},{112,80},{1... | collective-permute-start | bytes 786440 | tf_op jit(solution)/shard_map/ppermute | solution.py:16
  401.6 40.0 %collective-permute-start.7 = (f32[3,128]{1,0:T(4,128)S(1)}, f32[3,128]{1,0:T(4,128)S(1)}, u32[]{:S(2)}, u32[]{:S(2)}) collective-permute-start(f32[3,128]{1,0:T(4,128)S(1)} %fusion.67), channel_id=1, source_target_pairs={{0,64},{16,80},{32,96},{48,112},{64,0},{80,16},{96,32},{112,48},{1... | collective-permute-start | bytes 4616 | tf_op jit(solution)/shard_map/ppermute | solution.py:16
  438.2 10.8 %collective-permute-start.8 = (f32[128,512]{1,0:T(8,128)S(1)}, f32[128,512]{1,0:T(8,128)S(1)}, u32[]{:S(2)}, u32[]{:S(2)}) collective-permute-start(f32[128,512]{1,0:T(8,128)S(1)} %fusion.29), channel_id=1, source_target_pairs={{0,64},{16,80},{32,96},{48,112},{64,0},{80,16},{96,32},{112,48},{1... | collective-permute-start | bytes 786440 | tf_op jit(solution)/shard_map/ppermute | solution.py:16
  441.6 10.5 %collective-permute-start.6 = (f32[128,512]{1,0:T(8,128)S(1)}, f32[128,512]{1,0:T(8,128)S(1)}, u32[]{:S(2)}, u32[]{:S(2)}) collective-permute-start(f32[128,512]{1,0:T(8,128)S(1)} %convolution_multiply_fusion.1), channel_id=1, source_target_pairs={{0,64},{16,80},{32,96},{48,112},{64,0},{80,16},{96,32},{112,48},{1... | collective-permute-start | bytes 786440 | tf_op jit(solution)/shard_map/ppermute | solution.py:16
Sparse Core Ops, SparseCore 0:
  88.6 113.4 all-reduce.2
  233.4 115.8 all-reduce.4
where the time goes:
time: 496 us; the launch traced here: 489 us
  waiting for transfers between devices  206 us (42%)
  other arithmetic  101 us (20%)
  blocking collectives  63.6 us (13%)
  matrix products  62.6 us (13%)
  starting transfers between devices  29.9 us (6%)
  between operations  20.8 us (4%)
    psum x1, waiting for transfers between devices, local(): projected = lax.psum(jnp.dot(basis.T, own_omega, precision=HIGH), 'col')  112 us
    psum x1, waiting for transfers between devices, local(): picked, spots = lax.psum((part_picked, part_spots), 'col')  72.7 us
    another operation x12, other arithmetic, ridge_fit(): factor = jnp.linalg.cholesky(gram + shift * ident)  49.6 us
    another operation x8, other arithmetic, ridge_fit(): return jax.scipy.linalg.cho_solve((factor, True), picked)  41.9 us
    dot_general x2, matrix products, omega_rows(): counted = jnp.dot(row_bits, col_bits, precision=HIGH)  33.3 us
    ppermute x9, starting transfers between devices, swapped(): return lax.ppermute(value, axis, pairs)  29.8 us
    psum x1, blocking collectives, local(): picked, spots = lax.psum((part_picked, part_spots), 'col')  25.2 us
    all_gather x1, blocking collectives, local(): distant_points = lax.all_gather(points, 'col', axis=1, tiled=True)  23.8 us
  transfers between devices with their start and end apart: 11, of which 8 were waited for; matrix products, arithmetic and copies ran while one was open for 8% of the time, Pallas kernels for 0%

commit v1 on v0

--- a/solution.py
+++ b/solution.py
@@ -52,8 +52,11 @@
     bit_count = NTOTAL.bit_length() - 1
     tags = jnp.stack([point_ids, signs])
     own_omega = omega_rows(tags, hadamard_sample_rows, bit_count)
-    distant_points = lax.all_gather(points, "col", axis=1, tiled=True)
-    far_tags = lax.all_gather(tags, "col", axis=1, tiled=True)
+    distant_points, far_tags = jnp.split(
+        lax.all_gather(jnp.concatenate([points, tags], axis=0), "col", axis=1, tiled=True),
+        [points.shape[0]],
+        axis=0,
+    )
     block_omega = omega_rows(far_tags, hadamard_sample_rows, bit_count).astype(jnp.bfloat16)
     tile = kernel_tile(points, distant_points).astype(jnp.bfloat16)
     near = jnp.dot(tile, block_omega, preferred_element_type=jnp.float32)

time: 496 us -> 473 us (0.954)
  blocking collectives: 63.6 us -> 47.8 us
  matrix products: 62.6 us -> 55.8 us
    all_gather x2 -> x1, blocking collectives: 38.4 us -> 23.8 us  [local(): lax.all_gather(jnp.concatenate([points, tags], axis=0), 'col', axis=1, ti...]
    dot_general x2, matrix products: 33.3 us -> 26.3 us  [omega_rows(): counted = jnp.dot(row_bits, col_bits, precision=HIGH)]
where the time goes in v1:
time: 473 us; the launch traced here: 468 us
  waiting for transfers between devices  207 us (44%)
  other arithmetic  102 us (22%)
  matrix products  55.8 us (12%)
  blocking collectives  47.8 us (10%)
  starting transfers between devices  29.6 us (6%)
  between operations  20.6 us (4%)
    psum x1, waiting for transfers between devices, local(): projected = lax.psum(jnp.dot(basis.T, own_omega, precision=HIGH), 'col')  112 us
    psum x1, waiting for transfers between devices, local(): picked, spots = lax.psum((part_picked, part_spots), 'col')  73.9 us
    another operation x12, other arithmetic, ridge_fit(): factor = jnp.linalg.cholesky(gram + shift * ident)  49.6 us
    another operation x8, other arithmetic, ridge_fit(): return jax.scipy.linalg.cho_solve((factor, True), picked)  41.9 us
    ppermute x9, starting transfers between devices, swapped(): return lax.ppermute(value, axis, pairs)  29.5 us
    dot_general x2, matrix products, omega_rows(): counted = jnp.dot(row_bits, col_bits, precision=HIGH)  26.3 us
    psum x1, blocking collectives, local(): picked, spots = lax.psum((part_picked, part_spots), 'col')  23.9 us
    all_gather x1, blocking collectives, local(): lax.all_gather(jnp.concatenate([points, tags], axis=0), 'col', axis=1, ti...  23.8 us
  transfers between devices with their start and end apart: 11, of which 8 were waited for; matrix products, arithmetic and copies ran while one was open for 8% of the time, Pallas kernels for 0%

profile of v1, /device:TPU:2, one launch (start us, length us, event | category | flops | bytes accessed | tf_op | source)
XLA Modules:
  0.0 467.6 jit_solution(16658454850506779742)
XLA Ops:
  7.3 0.8 fusion.202
  8.1 0.7 add_convert_fusion
  8.8 0.7 pad_maximum_fusion.9
  9.5 23.8 %all_gather.3 = f32[5,8192]{1,0:T(8,128)S(1)} all-gather(f32[5,512]{1,0:T(8,128)S(1)} %pad_maximum_fusion.9), channel_id=1, replica_groups=mesh['leaf'=32,'col'=16] {'col'}, dimensions={1}, use_global_device_ids=true | all-gather | bytes 174080 | tf_op jit(solution)/shard_map/all_gather | solution.py:56
  33.5 0.7 compare_reduce_fusion
  34.2 1.7 fusion.203
  36.0 0.7 compare_convert_fusion.9
  36.6 0.8 fusion.166
  37.4 22.2 %multiply_convert_fusion = bf16[8192,512]{1,0:T(8,128)(2,1)S(1)} fusion(f32[8192]{0:T(1024)S(1)} %bitcast.148, f32[20]{0:T(128)} %constant.272, f32[20]{0:T(128)} %constant.261, f32[8192]{0:T(1024)S(1)} %bitcast.149, s32[20]{0:T(128)} %constant.260.clone, s32[512]{0:T(512)} %param.17, pred[512]{0:T(512)(128)(4,1)S(1)} %compare_reduce_fusion), kind=kOutput, calls=%fused_computation | convolution fusion | flops 1047187456 | bytes 8456944 | tf_op jit(solution)/shard_map/dot_general | solution.py:23
  59.7 6.7 %fusion.8 = f32[512,512]{1,0:T(8,128)S(1)} fusion(bf16[8192,512]{1,0:T(8,128)(2,1)S(1)} %multiply_convert_fusion, f32[8192]{0:T(1024)S(1)} %bitcast.146, f32[512]{0:T(512)S(1)} %bitcast.155, f32[8192]{0:T(1024)S(1)} %bitcast.147, f32[512]{0:T(512)S(1)} %bitcast.154, f32[8192]{0:T(1024)S(1)} %bitcast.145, f32[512]{0:T(512)S(1)} %bitcast.153, ...), kind=kOutput, calls=%fused_computation.13 | convolution fusion | flops 4337434624 | bytes 10065920 | tf_op jit(solution)/shard_map/dot_general | solution.py:62
  66.4 1.2 convolution_multiply_fusion.3
  67.9 23.9 %psum.22 = f32[3,128]{1,0:T(4,128)S(1)} all-reduce(f32[3,128]{1,0:T(4,128)S(1)} %convolution_bitcast_fusion), channel_id=1, replica_groups=mesh['leaf'=32,'col'=16] {'col'}, use_global_device_ids=true, to_apply=%region_4.8 | all-reduce | flops 384 | bytes 3072 | tf_op jit(solution)/shard_map/psum | solution.py:71
  91.9 2.6 collective-permute-start.1
  95.3 0.6 compare_convert_fusion.6
  96.6 0.6 compare_convert_fusion.7
  97.2 4.1 fusion.56
  101.8 0.7 compare_convert_fusion.4
  103.1 0.7 compare_convert_fusion.3
  103.8 0.7 compare_convert_fusion.1
  104.5 0.7 compare_convert_fusion.2
  105.1 0.7 compare_convert_fusion
  107.2 73.9 %all-reduce.3.cloned.1.call-done = f32[128,512]{1,0:T(8,128)} async-done(((f32[128,512]{1,0:T(8,128)}), f32[128,512]{1,0:T(8,128)}) %all-reduce.3.cloned.1.call-update) | async-done | bytes 262160 | tf_op jit(solution)/shard_map/psum | solution.py:71
  181.1 2.1 select_reduce_fusion.7
  184.0 11.7 %cholesky.74 = f32[128,128]{1,0:T(8,128)S(1)} custom-call(f32[128,128]{1,0:T(8,128)S(1)} %fusion.96), custom_call_target="Cholesky" | custom-call | tf_op jit(solution)/shard_map/jit(cholesky)/cholesky | solution.py:40
  195.7 0.6 compare_reduce_fusion.4
  196.4 0.7 fusion.73
  197.0 9.8 %custom-call.10 = f32[1,128,128]{1,2,0:T(8,128)S(1)} custom-call(f32[1,128,128]{2,1,0:T(8,128)S(1)} %fusion.73), custom_call_target="InvertDiagBlocksLowerTriangular" | custom-call | tf_op jit(solution)/shard_map/jit(_cho_solve)/triangular_solve | solution.py:41
  206.9 1.4 fusion.94
  208.6 2.1 fusion.204
  210.7 1.8 fusion.9
  212.7 4.0 collective-permute-start.4
  216.7 111.8 %all-reduce.5.cloned.1.call-done = f32[128,512]{1,0:T(8,128)} async-done(((f32[128,512]{1,0:T(8,128)}), f32[128,512]{1,0:T(8,128)}) %all-reduce.5.cloned.1.call-update) | async-done | bytes 262160 | tf_op jit(solution)/shard_map/psum | solution.py:75
  328.5 2.5 collective-permute-start.2
  331.0 3.4 collective-permute-start
  334.4 5.4 %collective-permute-done.2 = f32[128,512]{1,0:T(8,128)S(1)} collective-permute-done((f32[128,512]{1,0:T(8,128)}, f32[128,512]{1,0:T(8,128)S(1)}, u32[]{:S(2)}, u32[]{:S(2)}) %collective-permute-start.2) | collective-permute-done | bytes 262176 | tf_op jit(solution)/shard_map/ppermute | solution.py:16
  339.8 1.0 broadcast_select_fusion.1
  340.8 3.5 collective-permute-done
  344.3 1.5 subtract_multiply_fusion.4
  346.6 1.0 select_reduce_fusion.6
  348.5 11.7 %cholesky.85 = f32[128,128]{1,0:T(8,128)S(1)} custom-call(f32[128,128]{1,0:T(8,128)S(1)} %fusion.91), custom_call_target="Cholesky" | custom-call | tf_op jit(solution)/shard_map/jit(cholesky)/cholesky | solution.py:40
  360.2 0.6 compare_reduce_fusion.3
  360.9 0.7 fusion.74
  361.5 9.8 %custom-call.11 = f32[1,128,128]{1,2,0:T(8,128)S(1)} custom-call(f32[1,128,128]{2,1,0:T(8,128)S(1)} %fusion.74), custom_call_target="InvertDiagBlocksLowerTriangular" | custom-call | tf_op jit(solution)/shard_map/jit(_cho_solve)/triangular_solve | solution.py:41
  373.2 4.0 collective-permute-start.5
  377.2 3.4 collective-permute-start.3
  380.8 3.6 collective-permute-start.7
  384.4 1.3 collective-permute-done.5
  385.7 3.7 collective-permute-done.3
  390.8 1.0 select_reduce_fusion.5
  392.6 11.7 %cholesky.96 = f32[128,128]{1,0:T(8,128)S(1)} custom-call(f32[128,128]{1,0:T(8,128)S(1)} %fusion.86), custom_call_target="Cholesky" | custom-call | tf_op jit(solution)/shard_map/jit(cholesky)/cholesky | solution.py:40
  404.4 0.6 compare_reduce_fusion.2
  405.0 0.7 fusion.75
  405.7 9.8 %custom-call.12 = f32[1,128,128]{1,2,0:T(8,128)S(1)} custom-call(f32[1,128,128]{2,1,0:T(8,128)S(1)} %fusion.75), custom_call_target="InvertDiagBlocksLowerTriangular" | custom-call | tf_op jit(solution)/shard_map/jit(_cho_solve)/triangular_solve | solution.py:41
  417.3 3.4 collective-permute-start.8
  420.8 2.6 collective-permute-start.6
  423.4 4.7 %collective-permute-done.8 = f32[128,512]{1,0:T(8,128)S(1)} collective-permute-done((f32[128,512]{1,0:T(8,128)S(1)}, f32[128,512]{1,0:T(8,128)S(1)}, u32[]{:S(2)}, u32[]{:S(2)}) %collective-permute-start.8) | collective-permute-done | bytes 262176 | tf_op jit(solution)/shard_map/ppermute | solution.py:16
  428.2 3.1 collective-permute-done.6
  432.6 1.0 select_reduce_fusion.4
  434.4 11.7 %cholesky.107 = f32[128,128]{1,0:T(8,128)S(1)} custom-call(f32[128,128]{1,0:T(8,128)S(1)} %fusion.81), custom_call_target="Cholesky" | custom-call | tf_op jit(solution)/shard_map/jit(cholesky)/cholesky | solution.py:40
  446.2 0.6 compare_reduce_fusion.1
  446.8 0.7 fusion.76
  447.5 9.8 %custom-call.13 = f32[1,128,128]{1,2,0:T(8,128)S(1)} custom-call(f32[1,128,128]{2,1,0:T(8,128)S(1)} %fusion.76), custom_call_target="InvertDiagBlocksLowerTriangular" | custom-call | tf_op jit(solution)/shard_map/jit(_cho_solve)/triangular_solve | solution.py:41
  459.2 0.7 dynamic_slice.64
  459.8 0.7 dynamic_slice.65
  (74 shorter events, 12.0 us)
Async XLA Ops:
  7.2 173.9 %all-reduce.3.cloned.1.call-start = ((), (), s32[]{:S(2)}) async-start(), calls=%async_computation | async-start | bytes 524288 | tf_op jit(solution)/shard_map/psum | solution.py:71
  37.4 22.2 %copy-start.5 = (bf16[512,512]{1,0:T(8,128)(2,1)S(1)}, bf16[512,512]{1,0:T(8,128)(2,1)}, u32[]{:S(2)}) copy-start(bf16[512,512]{1,0:T(8,128)(2,1)} %param.18) | copy-start | bytes 1572868
  59.6 8.1 %copy-start.1 = (f32[3,512]{1,0:T(4,128)S(1)}, f32[3,512]{1,0:T(4,128)}, u32[]{:S(2)}) copy-start(f32[3,512]{1,0:T(4,128)} %param.14) | copy-start | bytes 18436
  59.6 35.6 %copy-start.2 = (s32[512]{0:T(512)S(1)}, s32[512]{0:T(512)}, u32[]{:S(2)}) copy-start(s32[512]{0:T(512)} %param.15) | copy-start | bytes 6148
  59.6 35.6 %copy-start.3 = (s32[512]{0:T(512)S(1)}, s32[512]{0:T(512)}, u32[]{:S(2)}) copy-start(s32[512]{0:T(512)} %param.16) | copy-start | bytes 6148
  59.6 37.5 %copy-start.4 = (s32[512]{0:T(512)S(1)}, s32[512]{0:T(512)}, u32[]{:S(2)}) copy-start(s32[512]{0:T(512)} %param.17) | copy-start | bytes 6148
  59.7 37.5 %copy-start.6 = (s32[20]{0:T(128)S(1)}, s32[20]{0:T(128)}, u32[]{:S(2)}) copy-start(s32[20]{0:T(128)} %constant.260.clone) | copy-start | bytes 244
  67.7 260.9 %all-reduce.5.cloned.1.call-start = ((), (), s32[]{:S(2)}) async-start(), calls=%async_computation.1 | async-start | bytes 524288 | tf_op jit(solution)/shard_map/psum | solution.py:75
  91.9 15.3 %collective-permute-start.1 = (f32[3,128]{1,0:T(4,128)S(1)}, f32[3,128]{1,0:T(4,128)S(1)}, u32[]{:S(2)}, u32[]{:S(2)}) collective-permute-start(f32[3,128]{1,0:T(4,128)S(1)} %psum.22), channel_id=1, source_target_pairs={{0,16},{16,0},{32,48},{48,32},{64,80},{80,64},{96,112},{112,96},{1... | collective-permute-start | bytes 4616 | tf_op jit(solution)/shard_map/ppermute | solution.py:16
  181.1 164.8 %copy-start = (f32[128,512]{1,0:T(8,128)S(1)}, f32[128,512]{1,0:T(8,128)}, u32[]{:S(2)}) copy-start(f32[128,512]{1,0:T(8,128)} %all-reduce.3.cloned.1.call-done) | copy-start | bytes 786436
  212.7 121.7 %collective-permute-start.4 = (f32[3,128]{1,0:T(4,128)S(1)}, f32[3,128]{1,0:T(4,128)S(1)}, u32[]{:S(2)}, u32[]{:S(2)}) collective-permute-start(f32[3,128]{1,0:T(4,128)S(1)} %fusion.68), channel_id=1, source_target_pairs={{0,32},{16,48},{32,0},{48,16},{64,96},{80,112},{96,64},{112,80},{1... | collective-permute-start | bytes 4616 | tf_op jit(solution)/shard_map/ppermute | solution.py:16
  328.5 11.3 %collective-permute-start.2 = (f32[128,512]{1,0:T(8,128)}, f32[128,512]{1,0:T(8,128)S(1)}, u32[]{:S(2)}, u32[]{:S(2)}) collective-permute-start(f32[128,512]{1,0:T(8,128)} %all-reduce.5.cloned.1.call-done), channel_id=1, source_target_pairs={{0,16},{16,0},{32,48},{48,32},{64,80},{80,64},{96,112},{112,96},{1... | collective-permute-start | bytes 786440 | tf_op jit(solution)/shard_map/ppermute | solution.py:16
  331.0 13.3 %collective-permute-start = (f32[128,512]{1,0:T(8,128)}, f32[128,512]{1,0:T(8,128)S(1)}, u32[]{:S(2)}, u32[]{:S(2)}) collective-permute-start(f32[128,512]{1,0:T(8,128)} %all-reduce.3.cloned.1.call-done), channel_id=1, source_target_pairs={{0,16},{16,0},{32,48},{48,32},{64,80},{80,64},{96,112},{112,96},{1... | collective-permute-start | bytes 786440 | tf_op jit(solution)/shard_map/ppermute | solution.py:16
  373.2 12.5 %collective-permute-start.5 = (f32[128,512]{1,0:T(8,128)S(1)}, f32[128,512]{1,0:T(8,128)S(1)}, u32[]{:S(2)}, u32[]{:S(2)}) collective-permute-start(f32[128,512]{1,0:T(8,128)S(1)} %fusion.27), channel_id=1, source_target_pairs={{0,32},{16,48},{32,0},{48,16},{64,96},{80,112},{96,64},{112,80},{1... | collective-permute-start | bytes 786440 | tf_op jit(solution)/shard_map/ppermute | solution.py:16
  377.2 12.3 %collective-permute-start.3 = (f32[128,512]{1,0:T(8,128)S(1)}, f32[128,512]{1,0:T(8,128)S(1)}, u32[]{:S(2)}, u32[]{:S(2)}) collective-permute-start(f32[128,512]{1,0:T(8,128)S(1)} %convolution_multiply_fusion.2), channel_id=1, source_target_pairs={{0,32},{16,48},{32,0},{48,16},{64,96},{80,112},{96,64},{112,80},{1... | collective-permute-start | bytes 786440 | tf_op jit(solution)/shard_map/ppermute | solution.py:16
  380.8 40.0 %collective-permute-start.7 = (f32[3,128]{1,0:T(4,128)S(1)}, f32[3,128]{1,0:T(4,128)S(1)}, u32[]{:S(2)}, u32[]{:S(2)}) collective-permute-start(f32[3,128]{1,0:T(4,128)S(1)} %fusion.69), channel_id=1, source_target_pairs={{0,64},{16,80},{32,96},{48,112},{64,0},{80,16},{96,32},{112,48},{1... | collective-permute-start | bytes 4616 | tf_op jit(solution)/shard_map/ppermute | solution.py:16
  417.3 10.8 %collective-permute-start.8 = (f32[128,512]{1,0:T(8,128)S(1)}, f32[128,512]{1,0:T(8,128)S(1)}, u32[]{:S(2)}, u32[]{:S(2)}) collective-permute-start(f32[128,512]{1,0:T(8,128)S(1)} %fusion.31), channel_id=1, source_target_pairs={{0,64},{16,80},{32,96},{48,112},{64,0},{80,16},{96,32},{112,48},{1... | collective-permute-start | bytes 786440 | tf_op jit(solution)/shard_map/ppermute | solution.py:16
  420.8 10.5 %collective-permute-start.6 = (f32[128,512]{1,0:T(8,128)S(1)}, f32[128,512]{1,0:T(8,128)S(1)}, u32[]{:S(2)}, u32[]{:S(2)}) collective-permute-start(f32[128,512]{1,0:T(8,128)S(1)} %convolution_multiply_fusion.1), channel_id=1, source_target_pairs={{0,64},{16,80},{32,96},{48,112},{64,0},{80,16},{96,32},{112,48},{1... | collective-permute-start | bytes 786440 | tf_op jit(solution)/shard_map/ppermute | solution.py:16
Sparse Core Ops, SparseCore 0:
  67.8 113.2 all-reduce.2
  212.6 115.8 all-reduce.4
